TPU v7x, 32 devices: a whole 2x2x4 slice. The times are simulated.
32 devices in a mesh: parts: 2 (over y), sub: 4 (over z), row: 2 (over x), col: 2 (over core).
Axes of the slice: x: 2, y: 2, z: 4, core: 2. Of those that a mesh axis runs over, the one named last changes fastest.
Arguments:
- loads: float32 [8, 32, 1024], P(('parts', 'sub'), 'col'), parts along dimension 0, may hold values from -6 to 6
- weights: float32 [8, 1024], P(('parts', 'sub')), parts along dimension 0, may hold values from 0.25 to 4
- dual_ops: bfloat16 [8, 2048, 2048], P(('parts', 'sub'), 'row'), parts along dimension 0, as said below
- corner_maps: bfloat16 [8, 24, 2048], P(('parts', 'sub'), None, 'row'), parts along dimension 0, may hold values from -0.25 to 0.25
- coarse_inverse: float32 [96, 48], P('parts'), parts along dimension 0, as said below
- corner_ids: int32 [8, 24], P('parts'), parts along dimension 0, may hold values from 0 to 47, as said below
- iface_sizes: int32 [8], P('parts'), parts along dimension 0, may hold values from 512 to 1024, as said below
- left_partner: int32 [8, 1024], P(('parts', 'sub')), parts along dimension 0, may hold values from 0 to 1023, as said below
- right_partner: int32 [8, 1024], P(('parts', 'sub')), parts along dimension 0, may hold values from 0 to 1023, as said below
Outputs:
- solution: float32 [8, 32, 1024], P(('parts', 'sub'), 'col'), parts along dimension 0
- residual: float32 [8, 32, 1024], P(('parts', 'sub'), 'col'), parts along dimension 0
There are 2 independent parts, one for each index of `parts`. A program takes and returns all parts, laid end to end along the dimension named above; each array names one. Nothing has to cross between parts.
Inputs may be any that keep to these rules, and one draw needn't show every extreme that they name: Global indices 24/2 * s to 24/2 * s + 24/2 - 1 are the corners of the interface between s and s+1; the first half of subdomain s's corner_ids is a permutation of those of interface s-1, the second half a permutation of those of interface s. `left_partner`: each row s is a permutation that maps the slots below iface_sizes[s-1] onto slots below it. `right_partner`: each row s is a permutation that maps the slots below iface_sizes[s] onto slots below it, and is the inverse of left_partner[s+1]. `dual_ops`: symmetric positive definite. `coarse_inverse`: symmetric positive definite. For each s < 2, one of iface_sizes[s] and iface_sizes[s + 2] is 896 or more and the other 640 or less.
All inputs are finite; a program needn't handle non-finite values.
Results may differ from a plain program's by a relative error of at most 0.015.
Values may be sent and summed in bfloat16 or wider, within the bound.
No kernel may reach another device: no remote copies, remote signals or barrier semaphores. Data moves between devices by JAX's collectives and lax.ppermute only.
A program may use at most 64 MiB of HBM per device.

v0:
```python
import jax
import jax.numpy as jnp
from jax import lax
from jax.sharding import PartitionSpec as P

TILE = 128
ITERS = 2


def shifted(value, axis, steps):
    count = lax.axis_size(axis)
    pairs = [(source, (source + steps) % count) for source in range(count)]
    return lax.ppermute(value, axis, pairs)


def inner(first, second, half):
    return jnp.sum(first[:, :half] * second[:, :half], axis=1)


def paired_totals(residual, precond, image, half):
    return lax.psum((inner(residual, precond, half), inner(precond, image, half)), "sub")


def tile_products(vector, rows_op, first_tile, last_tile, output):

    def one_tile(tile_at, acc):
        piece = lax.dynamic_slice_in_dim(rows_op, tile_at * TILE, TILE, 0)
        product = lax.dot_general(
            vector, piece, (((1,), (1,)), ((), ())), preferred_element_type=jnp.float32
        )
        return lax.dynamic_update_slice_in_dim(acc, product, tile_at * TILE, 1)

    return lax.fori_loop(first_tile, last_tile, one_tile, output)


def live_tiles(size_before, size_after, block_start, block, half):
    left_live = jnp.clip(size_before - block_start, 0, block)
    right_live = jnp.clip(size_after - (block_start - half), 0, block)
    live_cols = jnp.where(block_start < half, left_live, right_live)
    return (live_cols + TILE - 1) // TILE


def per_device(
    loads,
    weights,
    dual_ops,
    corner_maps,
    coarse_inverse,
    corner_ids,
    iface_sizes,
    left_partner,
    right_partner,
):
    half = loads.shape[2]
    block = dual_ops.shape[1]
    width = coarse_inverse.shape[0]
    subdomain = lax.axis_index("sub")
    count = lax.axis_size("sub")
    row_index = lax.axis_index("row")
    left_map = left_partner[0]
    right_map = right_partner[0]
    slots = jnp.arange(half, dtype=jnp.int32)
    size_before = iface_sizes[(subdomain + count - 1) % count]
    size_after = iface_sizes[subdomain]
    live_left = (slots < size_before).astype(jnp.float32)
    live_right = (right_map < size_after).astype(jnp.float32)
    columns = jnp.arange(width, dtype=jnp.int32)
    own_hot = (corner_ids[subdomain][:, None] == columns[None, :]).astype(jnp.float32)
    operator = dual_ops[0]
    coupling = corner_maps[0]
    block_start = row_index * block
    own_tiles = live_tiles(size_before, size_after, block_start, block, half)

    def apply_operator(vec):
        halfway = vec.astype(jnp.bfloat16)
        empty = jnp.zeros((halfway.shape[0], block), jnp.float32)
        local = tile_products(halfway, operator, jnp.int32(0), own_tiles, empty)
        own_slots = lax.dynamic_slice_in_dim(halfway, row_index * block, block, 1)
        corner = lax.dot_general(
            own_slots, coupling, (((1,), (1,)), ((), ())), preferred_element_type=jnp.float32
        )
        scattered = jnp.dot(corner, own_hot, precision=lax.Precision.HIGHEST)
        coarse = lax.psum(scattered, ("sub", "row"))
        solved = jnp.dot(coarse, coarse_inverse, precision=lax.Precision.HIGHEST)
        back = lax.dot_general(
            solved, own_hot, (((1,), (1,)), ((), ())), precision=lax.Precision.HIGHEST
        ).astype(jnp.bfloat16)
        united = local + jnp.dot(back, coupling, preferred_element_type=jnp.float32)
        whole = lax.all_gather(united.astype(jnp.bfloat16), "row", axis=1, tiled=True).astype(
            united.dtype
        )
        lower = whole[:, :half]
        upper = whole[:, half:]
        arrived_left = shifted(upper.astype(jnp.bfloat16), "sub", 1).astype(upper.dtype)
        arrived_right = shifted(lower.astype(jnp.bfloat16), "sub", -1).astype(lower.dtype)
        result_left = (lower + jnp.take(arrived_left, left_map, axis=1)) * live_left
        result_right = (upper + jnp.take(arrived_right, right_map, axis=1)) * live_right
        return jnp.concatenate([result_left, result_right], axis=1)

    received = (
        shifted(loads[0].astype(jnp.bfloat16), "sub", -1).astype(jnp.float32),
        shifted(weights.astype(jnp.bfloat16), "sub", -1).astype(weights.dtype),
    )
    right_load = jnp.take(received[0], right_map, axis=1) * live_right
    right_weight = jnp.take(received[1], right_map, axis=1)
    residual = jnp.concatenate([loads[0] * live_left, right_load], axis=1)
    scaling = jnp.concatenate([weights, right_weight], axis=1)
    solution = jnp.zeros_like(residual)
    precond = scaling * residual
    image = apply_operator(precond)
    gamma, delta = paired_totals(residual, precond, image, half)
    alpha = gamma / delta
    direction = precond
    along = image
    for step in range(ITERS):
        solution = solution + alpha[:, None] * direction
        residual = residual - alpha[:, None] * along
        if step + 1 < ITERS:
            precond = scaling * residual
            image = apply_operator(precond)
            gamma_next, delta = paired_totals(residual, precond, image, half)
            ratio = gamma_next / gamma
            alpha = gamma_next / (delta - ratio * gamma_next / alpha)
            direction = precond + ratio[:, None] * direction
            along = image + ratio[:, None] * along
            gamma = gamma_next
    return (solution[:, :half][None], residual[:, :half][None])


def solution(mesh):
    placed = (
        P(("parts", "sub"), "col", None),
        P(("parts", "sub"), None),
        P(("parts", "sub"), "row", None),
        P(("parts", "sub"), None, "row"),
        P("parts", None),
        P("parts", None),
        P("parts"),
        P(("parts", "sub"), None),
        P(("parts", "sub"), None),
    )
    return jax.shard_map(
        per_device,
        mesh=mesh,
        in_specs=placed,
        out_specs=(P(("parts", "sub"), "col", None), P(("parts", "sub"), "col", None)),
        check_vma=False,
    )
```

profile of v0, /device:TPU:0, one launch (start us, length us, event | category | flops | bytes accessed | tf_op | source)
XLA Modules:
  0.0 136.2 jit_solution(17909804324471528583)
XLA Ops:
  0.7 0.9 bitcast_convert_fusion
  1.5 5.1 %collective-permute-start.1 = (bf16[16,1024]{1,0:T(8,128)(2,1)S(1)}, bf16[16,1024]{1,0:T(8,128)(2,1)S(1)}, u32[]{:S(2)}, u32[]{:S(2)}) collective-permute-start(bf16[16,1024]{1,0:T(8,128)(2,1)S(1)} %bitcast_convert_fusion), channel_id=1, source_target_pairs={{0,12},{4,0},{8,4},{12,8},{1,13},{5,1},{9,5},{13,9},{2,14},{6,2},{... | collective-permute-start | bytes 98312 | tf_op jit(solution)/shard_map/ppermute | solution.py:13
  6.6 0.7 convert_element_type.71
  7.3 0.4 collective-permute-start
  7.8 0.7 compare_select_fusion
  8.4 0.7 fusion.36
  9.1 1.3 fusion.49
  10.5 1.3 fusion.35
  11.8 1.3 compare_convert_fusion
  13.1 0.8 bitcast_multiply_fusion.1
  14.0 0.7 fusion.40
  14.7 0.7 fusion.37
  16.7 4.5 %gather_fusion = f32[1024]{0:T(1024)S(1)} fusion(f32[1024]{0:T(1024)S(1)} %bitcast.80, s32[1024]{0:T(1024)S(1)} %broadcast_clamp_fusion), kind=kCustom, calls=%fused_computation.5 | custom fusion | bytes 12288 | tf_op jit(solution)/shard_map/jit(_take)/gather | solution.py:105
  21.5 2.8 %gather_fusion.1 = f32[1024,16]{1,0:T(8,128)S(1)} fusion(f32[16,1024]{0,1:T(8,128)S(1)} %copy.21, s32[1024]{0:T(1024)S(1)} %fusion.36), kind=kCustom, calls=%fused_computation.clone | custom fusion | bytes 135168 | tf_op jit(solution)/shard_map/jit(_take)/gather | solution.py:104
  24.5 10.4 %while.20 = (s32[]{:T(128)}, f32[16,1024]{1,0:T(8,128)S(1)}, s32[]{:T(128)}, bf16[1024,2048]{1,0:T(8,128)(2,1)}, bf16[16,2048]{1,0:T(8,128)(2,1)S(1)}, /*index=5*/s32[]{:T(128)}, s32[]{:T(128)}, s32[]{:T(128)}, s32[]{:T(128)}) while((s32[]{:T(128)}, f32[16,1024]{1,0:T(8,128)S(1)}, s32[]{:T(128)}, bf16[1024,2048]{1,0:T(8,128)(2,1)}, ...), condition=%wide.region_3.5_spmd, body=%wide.region_2.4_spmd.sunk | while | flops 8388614 | bytes 599179 | solution.py:33
  24.6 1.3 fusion.72
  25.9 1.3 fusion.72
  27.1 1.3 fusion.72
  28.4 1.3 fusion.72
  29.7 1.3 fusion.72
  31.0 1.3 fusion.72
  32.3 1.3 fusion.72
  33.6 1.3 fusion.72
  35.3 18.9 %psum.43 = f32[16,48]{1,0:T(8,128)S(1)} all-reduce(f32[16,48]{1,0:T(8,128)S(1)} %fusion.30), channel_id=1, replica_groups=mesh['parts'=2,'sub'=4,'row'=2,'col'=2] {'sub','row'}, use_global_device_ids=true, to_apply=%region_4.6 | all-reduce | flops 768 | bytes 6144 | tf_op jit(solution)/shard_map/psum | solution.py:83
  54.6 4.6 %all_gather.6 = bf16[16,2048]{1,0:T(8,128)(2,1)S(1)} all-gather(bf16[16,1024]{1,0:T(8,128)(2,1)S(1)} %fusion.6), channel_id=1, replica_groups=mesh['parts'=2,'sub'=4,'row'=2,'col'=2] {'row'}, dimensions={1}, use_global_device_ids=true | all-gather | bytes 98304 | tf_op jit(solution)/shard_map/all_gather | solution.py:89
  59.2 3.8 %collective-permute-start.3 = (bf16[16,1024]{1,0:T(8,128)(2,1)S(1)}, bf16[16,1024]{1,0:T(8,128)(2,1)S(1)}, u32[]{:S(2)}, u32[]{:S(2)}) collective-permute-start(bf16[16,1024]{1,0:T(8,128)(2,1)S(1)} %get-tuple-element.103), channel_id=1, source_target_pairs={{0,12},{4,0},{8,4},{12,8},{1,13},{5,1},{9,5},{13,9},{2,14},{6,2},{... | collective-permute-start | bytes 98312 | tf_op jit(solution)/shard_map/ppermute | solution.py:13
  63.1 1.9 %collective-permute-done.2 = bf16[16,1024]{1,0:T(8,128)(2,1)S(1)} collective-permute-done((bf16[16,1024]{1,0:T(8,128)(2,1)S(1)}, bf16[16,1024]{1,0:T(8,128)(2,1)S(1)}, u32[]{:S(2)}, u32[]{:S(2)}) %collective-permute-start.2) | collective-permute-done | bytes 32800 | tf_op jit(solution)/shard_map/ppermute | solution.py:13
  65.1 2.8 %gather_fusion.2 = f32[1024,16]{1,0:T(8,128)S(1)} fusion(f32[16,1024]{0,1:T(8,128)S(1)} %copy.23, s32[1024]{0:T(1024)S(1)} %fusion.37), kind=kCustom, calls=%fused_computation.1.clone | custom fusion | bytes 135168 | tf_op jit(solution)/shard_map/jit(_take)/gather | solution.py:96
  68.2 2.8 %gather_fusion.3 = f32[1024,16]{1,0:T(8,128)S(1)} fusion(f32[16,1024]{0,1:T(8,128)S(1)} %copy.25, s32[1024]{0:T(1024)S(1)} %fusion.36), kind=kCustom, calls=%fused_computation.2.clone | custom fusion | bytes 135168 | tf_op jit(solution)/shard_map/jit(_take)/gather | solution.py:97
  71.3 9.1 %all-reduce.1 = (f32[16]{0:T(128)S(1)}, f32[16]{0:T(128)S(1)}) all-reduce(f32[16]{0:T(128)S(1)} %get-tuple-element.64, f32[16]{0:T(128)S(1)} %get-tuple-element.63), channel_id=1, replica_groups=mesh['parts'=2,'sub'=4,'row'=2,'col'=2] {'sub'}, use_global_device_ids=true, to_apply=%region_1.3 | all-reduce | flops 32 | bytes 256 | tf_op jit(solution)/shard_map/psum | solution.py:21
  80.6 10.3 %while.21 = (s32[]{:T(128)}, f32[16,1024]{1,0:T(8,128)S(1)}, s32[]{:T(128)}, bf16[1024,2048]{1,0:T(8,128)(2,1)}, bf16[16,2048]{1,0:T(8,128)(2,1)S(1)}, /*index=5*/s32[]{:T(128)}, s32[]{:T(128)}, s32[]{:T(128)}, s32[]{:T(128)}) while((s32[]{:T(128)}, f32[16,1024]{1,0:T(8,128)S(1)}, s32[]{:T(128)}, bf16[1024,2048]{1,0:T(8,128)(2,1)}, ...), condition=%wide.region_10.12_spmd, body=%wide.region_9.11_spmd.sunk | while | flops 8388614 | bytes 599179 | solution.py:33
  80.6 1.3 fusion.75
  81.9 1.3 fusion.75
  83.2 1.3 fusion.75
  84.5 1.3 fusion.75
  85.8 1.3 fusion.75
  87.1 1.3 fusion.75
  88.4 1.3 fusion.75
  89.7 1.3 fusion.75
  91.0 0.2 fusion.29
  91.2 18.7 %psum.46 = f32[16,48]{1,0:T(8,128)S(1)} all-reduce(f32[16,48]{1,0:T(8,128)S(1)} %fusion.29), channel_id=1, replica_groups=mesh['parts'=2,'sub'=4,'row'=2,'col'=2] {'sub','row'}, use_global_device_ids=true, to_apply=%region_11.13 | all-reduce | flops 768 | bytes 6144 | tf_op jit(solution)/shard_map/psum | solution.py:83
  110.3 4.6 %all_gather.7 = bf16[16,2048]{1,0:T(8,128)(2,1)S(1)} all-gather(bf16[16,1024]{1,0:T(8,128)(2,1)S(1)} %fusion.7), channel_id=1, replica_groups=mesh['parts'=2,'sub'=4,'row'=2,'col'=2] {'row'}, dimensions={1}, use_global_device_ids=true | all-gather | bytes 98304 | tf_op jit(solution)/shard_map/all_gather | solution.py:89
  114.9 2.0 %collective-permute-start.4 = (bf16[16,1024]{1,0:T(8,128)(2,1)S(1)}, bf16[16,1024]{1,0:T(8,128)(2,1)S(1)}, u32[]{:S(2)}, u32[]{:S(2)}) collective-permute-start(bf16[16,1024]{1,0:T(8,128)(2,1)S(1)} %get-tuple-element.101), channel_id=1, source_target_pairs={{0,4},{4,8},{8,12},{12,0},{1,5},{5,9},{9,13},{13,1},{2,6},{6,10},{... | collective-permute-start | bytes 98312 | tf_op jit(solution)/shard_map/ppermute | solution.py:13
  117.0 1.9 %collective-permute-done.5 = bf16[16,1024]{1,0:T(8,128)(2,1)S(1)} collective-permute-done((bf16[16,1024]{1,0:T(8,128)(2,1)S(1)}, bf16[16,1024]{1,0:T(8,128)(2,1)S(1)}, u32[]{:S(2)}, u32[]{:S(2)}) %collective-permute-start.5) | collective-permute-done | bytes 32800 | tf_op jit(solution)/shard_map/ppermute | solution.py:13
  119.0 2.8 %gather_fusion.5 = f32[1024,16]{1,0:T(8,128)S(1)} fusion(f32[16,1024]{0,1:T(8,128)S(1)} %copy.29, s32[1024]{0:T(1024)S(1)} %fusion.36), kind=kCustom, calls=%fused_computation.4.clone | custom fusion | bytes 135168 | tf_op jit(solution)/shard_map/jit(_take)/gather | solution.py:97
  122.1 2.8 %gather_fusion.4 = f32[1024,16]{1,0:T(8,128)S(1)} fusion(f32[16,1024]{0,1:T(8,128)S(1)} %copy.27, s32[1024]{0:T(1024)S(1)} %fusion.37), kind=kCustom, calls=%fused_computation.3.clone | custom fusion | bytes 135168 | tf_op jit(solution)/shard_map/jit(_take)/gather | solution.py:96
  125.3 10.2 %all-reduce = (f32[16]{0:T(128)S(1)}, f32[16]{0:T(128)S(1)}) all-reduce(f32[16]{0:T(128)S(1)} %get-tuple-element.62, f32[16]{0:T(128)S(1)} %get-tuple-element.61), channel_id=1, replica_groups=mesh['parts'=2,'sub'=4,'row'=2,'col'=2] {'sub'}, use_global_device_ids=true, to_apply=%region_8.10 | all-reduce | flops 32 | bytes 256 | tf_op jit(solution)/shard_map/psum | solution.py:21
  135.4 0.7 fusion.16
  (55 shorter events, 3.5 us)
Async XLA Ops:
  0.6 34.3 %copy-start = (bf16[1,24,1024]{2,1,0:T(8,128)(2,1)S(1)}, bf16[1,24,1024]{2,1,0:T(8,128)(2,1)}, u32[]{:S(2)}) copy-start(bf16[1,24,1024]{2,1,0:T(8,128)(2,1)} %param.18) | copy-start | bytes 147460
  0.6 20.7 %copy-start.5 = (f32[1,1024]{1,0:T(1,128)S(1)}, f32[1,1024]{1,0:T(1,128)}, u32[]{:S(2)}) copy-start(f32[1,1024]{1,0:T(1,128)} %param.16) | copy-start | bytes 12292
  0.7 20.6 %copy-start.2 = (s32[1,1024]{1,0:T(1,128)S(1)}, s32[1,1024]{1,0:T(1,128)}, u32[]{:S(2)}) copy-start(s32[1,1024]{1,0:T(1,128)} %param.23) | copy-start | bytes 12292
  1.5 19.8 %collective-permute-start.1 = (bf16[16,1024]{1,0:T(8,128)(2,1)S(1)}, bf16[16,1024]{1,0:T(8,128)(2,1)S(1)}, u32[]{:S(2)}, u32[]{:S(2)}) collective-permute-start(bf16[16,1024]{1,0:T(8,128)(2,1)S(1)} %bitcast_convert_fusion), channel_id=1, source_target_pairs={{0,12},{4,0},{8,4},{12,8},{1,13},{5,1},{9,5},{13,9},{2,14},{6,2},{... | collective-permute-start | bytes 98312 | tf_op jit(solution)/shard_map/ppermute | solution.py:13
  7.3 9.4 %collective-permute-start = (bf16[1,1024]{1,0:T(2,128)(2,1)S(1)}, bf16[1,1024]{1,0:T(2,128)(2,1)S(1)}, u32[]{:S(2)}, u32[]{:S(2)}) collective-permute-start(bf16[1,1024]{1,0:T(2,128)(2,1)S(1)} %convert_element_type.71), channel_id=1, source_target_pairs={{0,12},{4,0},{8,4},{12,8},{1,13},{5,1},{9,5},{13,9},{2,14},{6,2},{... | collective-permute-start | bytes 6152 | tf_op jit(solution)/shard_map/ppermute | solution.py:13
  16.7 37.4 %copy-start.3 = (f32[48,48]{1,0:T(8,128)S(1)}, f32[48,48]{1,0:T(8,128)}, u32[]{:S(2)}) copy-start(f32[48,48]{1,0:T(8,128)} %param.19) | copy-start | bytes 27652
  16.7 46.3 %copy-start.4 = (s32[1,1024]{1,0:T(1,128)S(1)}, s32[1,1024]{1,0:T(1,128)}, u32[]{:S(2)}) copy-start(s32[1,1024]{1,0:T(1,128)} %param.22) | copy-start | bytes 12292
  24.5 46.7 %copy-start.1 = (f32[1,16,1024]{2,1,0:T(8,128)S(1)}, f32[1,16,1024]{2,1,0:T(8,128)}, u32[]{:S(2)}) copy-start(f32[1,16,1024]{2,1,0:T(8,128)} %param.15) | copy-start | bytes 196612
  59.2 5.7 %collective-permute-start.2 = (bf16[16,1024]{1,0:T(8,128)(2,1)S(1)}, bf16[16,1024]{1,0:T(8,128)(2,1)S(1)}, u32[]{:S(2)}, u32[]{:S(2)}) collective-permute-start(bf16[16,1024]{1,0:T(8,128)(2,1)S(1)} %get-tuple-element.102), channel_id=1, source_target_pairs={{0,4},{4,8},{8,12},{12,0},{1,5},{5,9},{9,13},{13,1},{2,6},{6,10},{... | collective-permute-start | bytes 98312 | tf_op jit(solution)/shard_map/ppermute | solution.py:13
  59.2 8.8 %collective-permute-start.3 = (bf16[16,1024]{1,0:T(8,128)(2,1)S(1)}, bf16[16,1024]{1,0:T(8,128)(2,1)S(1)}, u32[]{:S(2)}, u32[]{:S(2)}) collective-permute-start(bf16[16,1024]{1,0:T(8,128)(2,1)S(1)} %get-tuple-element.103), channel_id=1, source_target_pairs={{0,12},{4,0},{8,4},{12,8},{1,13},{5,1},{9,5},{13,9},{2,14},{6,2},{... | collective-permute-start | bytes 98312 | tf_op jit(solution)/shard_map/ppermute | solution.py:13
  114.9 3.9 %collective-permute-start.5 = (bf16[16,1024]{1,0:T(8,128)(2,1)S(1)}, bf16[16,1024]{1,0:T(8,128)(2,1)S(1)}, u32[]{:S(2)}, u32[]{:S(2)}) collective-permute-start(bf16[16,1024]{1,0:T(8,128)(2,1)S(1)} %get-tuple-element.100), channel_id=1, source_target_pairs={{0,12},{4,0},{8,4},{12,8},{1,13},{5,1},{9,5},{13,9},{2,14},{6,2},{... | collective-permute-start | bytes 98312 | tf_op jit(solution)/shard_map/ppermute | solution.py:13
  114.9 7.0 %collective-permute-start.4 = (bf16[16,1024]{1,0:T(8,128)(2,1)S(1)}, bf16[16,1024]{1,0:T(8,128)(2,1)S(1)}, u32[]{:S(2)}, u32[]{:S(2)}) collective-permute-start(bf16[16,1024]{1,0:T(8,128)(2,1)S(1)} %get-tuple-element.101), channel_id=1, source_target_pairs={{0,4},{4,8},{8,12},{12,0},{1,5},{5,9},{9,13},{13,1},{2,6},{6,10},{... | collective-permute-start | bytes 98312 | tf_op jit(solution)/shard_map/ppermute | solution.py:13
where the time goes:
time: 137 us; the launch traced here: 136 us
  blocking collectives  65.9 us (48%)
  matrix products  22.3 us (16%)
  local copies, waits for them, and re-layouts  22.1 us (16%)
  starting transfers between devices  11.4 us (8%)
  other arithmetic  8.41 us (6%)
  waiting for transfers between devices  3.74 us (3%)
  between operations  2.25 us (2%)
    psum x2, blocking collectives, apply_operator(): coarse = lax.psum(scattered, ('sub', 'row'))  37.5 us
    dot_general x16, matrix products, one_tile(): lax.dot_general(vector, piece, (((1,), (1,)), ((), ())), preferred_elemen...  20.7 us
    psum x2, blocking collectives, paired_totals(): lax.psum((inner(residual, precond, half), inner(precond, image, half)), '...  19.2 us
    ppermute x6, starting transfers between devices, shifted(): return lax.ppermute(value, axis, pairs)  11.4 us
    all_gather x2, blocking collectives, apply_operator(): lax.all_gather(united.astype(jnp.bfloat16), 'row', axis=1, tiled=True)  9.15 us
    gather x4, local copies, waits for them, and re-layouts, apply_operator(): jnp.take(arrived_right, right_map, axis=1)  5.95 us
    gather x4, local copies, waits for them, and re-layouts, apply_operator(): result_left = (lower + jnp.take(arrived_left, left_map, axis=1)) * live_left  5.95 us
    gather x1, local copies, waits for them, and re-layouts, per_device(): right_weight = jnp.take(received[1], right_map, axis=1)  4.53 us
  transfers between devices with their start and end apart: 6, of which 2 were waited for; matrix products, arithmetic and copies ran while one was open for 14% of the time, Pallas kernels for 0%

commit v1 on v0

--- a/solution.py
+++ b/solution.py
@@ -80,7 +80,7 @@
             own_slots, coupling, (((1,), (1,)), ((), ())), preferred_element_type=jnp.float32
         )
         scattered = jnp.dot(corner, own_hot, precision=lax.Precision.HIGHEST)
-        coarse = lax.psum(scattered, ("sub", "row"))
+        coarse = lax.psum(lax.psum(scattered, "row"), "sub")
         solved = jnp.dot(coarse, coarse_inverse, precision=lax.Precision.HIGHEST)
         back = lax.dot_general(
             solved, own_hot, (((1,), (1,)), ((), ())), precision=lax.Precision.HIGHEST

time: 137 us -> 131 us (0.956)
  blocking collectives: 65.9 us -> 59 us
    psum x2 -> x4, blocking collectives: 37.5 us -> 29.9 us  [apply_operator(): coarse = lax.psum(lax.psum(scattered, 'row'), 'sub')]
  transfers between devices with their start and end apart: 6 -> 6, of which waited for: 2 -> 2; matrix products, arithmetic and copies ran while one was open for 14% -> 15% of each run, Pallas kernels for 0% -> 0%
where the time goes in v1:
time: 131 us; the launch traced here: 129 us
  blocking collectives  59 us (45%)
  matrix products  22.3 us (17%)
  local copies, waits for them, and re-layouts  22.1 us (17%)
  starting transfers between devices  11.4 us (9%)
  other arithmetic  8.41 us (6%)
  waiting for transfers between devices  3.74 us (3%)
  between operations  2.24 us (2%)
    psum x4, blocking collectives, apply_operator(): coarse = lax.psum(lax.psum(scattered, 'row'), 'sub')  29.9 us
    dot_general x16, matrix products, one_tile(): lax.dot_general(vector, piece, (((1,), (1,)), ((), ())), preferred_elemen...  20.7 us
    psum x2, blocking collectives, paired_totals(): lax.psum((inner(residual, precond, half), inner(precond, image, half)), '...  19.9 us
    ppermute x6, starting transfers between devices, shifted(): return lax.ppermute(value, axis, pairs)  11.4 us
    all_gather x2, blocking collectives, apply_operator(): lax.all_gather(united.astype(jnp.bfloat16), 'row', axis=1, tiled=True)  9.15 us
    gather x4, local copies, waits for them, and re-layouts, apply_operator(): jnp.take(arrived_right, right_map, axis=1)  5.95 us
    gather x4, local copies, waits for them, and re-layouts, apply_operator(): result_left = (lower + jnp.take(arrived_left, left_map, axis=1)) * live_left  5.95 us
    gather x1, local copies, waits for them, and re-layouts, per_device(): right_weight = jnp.take(received[1], right_map, axis=1)  4.53 us
  transfers between devices with their start and end apart: 6, of which 2 were waited for; matrix products, arithmetic and copies ran while one was open for 15% of the time, Pallas kernels for 0%

profile of v1, /device:TPU:0, one launch (start us, length us, event | category | flops | bytes accessed | tf_op | source)
XLA Modules:
  0.0 129.2 jit_solution(6204381350841478852)
XLA Ops:
  0.7 0.9 bitcast_convert_fusion
  1.5 5.1 %collective-permute-start.1 = (bf16[16,1024]{1,0:T(8,128)(2,1)S(1)}, bf16[16,1024]{1,0:T(8,128)(2,1)S(1)}, u32[]{:S(2)}, u32[]{:S(2)}) collective-permute-start(bf16[16,1024]{1,0:T(8,128)(2,1)S(1)} %bitcast_convert_fusion), channel_id=1, source_target_pairs={{0,12},{4,0},{8,4},{12,8},{1,13},{5,1},{9,5},{13,9},{2,14},{6,2},{... | collective-permute-start | bytes 98312 | tf_op jit(solution)/shard_map/ppermute | solution.py:13
  7.8 0.7 compare_select_fusion
  8.4 0.7 fusion.36
  9.1 1.3 %fusion.49 = (s32[1]{0:T(128)}, s32[1]{0:T(128)}) fusion(s32[4]{0:T(128)} %param.21, s32[]{:T(128)S(6)} %select_n.67, s32[]{:T(128)S(6)} %select_n.63), kind=kLoop, calls=%fused_computation.93 | loop fusion | bytes 24 | tf_op jit(solution)/shard_map/dynamic_slice | solution.py:64
  10.5 1.3 %fusion.35 = (f32[1024]{0:T(1024)S(1)}, pred[1024]{0:T(1024)(128)(4,1)S(1)}) fusion(s32[]{:T(128)} %bitcast.3, s32[1024]{0:T(1024)} %bitcast.83), kind=kLoop, calls=%fused_computation.78 | loop fusion | flops 8192 | bytes 9220 | tf_op jit(solution)/shard_map/convert_element_type | solution.py:65
  11.8 1.3 %compare_convert_fusion = f32[1,1024]{1,0:T(1,128)S(1)} fusion(s32[1,1024]{1,0:T(1,128)} %param.23, s32[]{:T(128)} %bitcast.11), kind=kLoop, calls=%fused_computation.65 | loop fusion | flops 2048 | bytes 8196 | tf_op jit(solution)/shard_map/mul | solution.py:104
  13.1 0.8 bitcast_multiply_fusion.1
  14.0 0.7 fusion.40
  14.7 0.7 fusion.37
  16.7 4.5 %gather_fusion = f32[1024]{0:T(1024)S(1)} fusion(f32[1024]{0:T(1024)S(1)} %bitcast.80, s32[1024]{0:T(1024)S(1)} %broadcast_clamp_fusion), kind=kCustom, calls=%fused_computation.5 | custom fusion | bytes 12288 | tf_op jit(solution)/shard_map/jit(_take)/gather | solution.py:105
  21.5 2.8 %gather_fusion.1 = f32[1024,16]{1,0:T(8,128)S(1)} fusion(f32[16,1024]{0,1:T(8,128)S(1)} %copy.21, s32[1024]{0:T(1024)S(1)} %fusion.36), kind=kCustom, calls=%fused_computation.clone | custom fusion | bytes 135168 | tf_op jit(solution)/shard_map/jit(_take)/gather | solution.py:104
  24.5 10.4 %while.20 = (s32[]{:T(128)}, f32[16,1024]{1,0:T(8,128)S(1)}, s32[]{:T(128)}, bf16[1024,2048]{1,0:T(8,128)(2,1)}, bf16[16,2048]{1,0:T(8,128)(2,1)S(1)}, /*index=5*/s32[]{:T(128)}, s32[]{:T(128)}, s32[]{:T(128)}, s32[]{:T(128)}) while((s32[]{:T(128)}, f32[16,1024]{1,0:T(8,128)S(1)}, s32[]{:T(128)}, bf16[1024,2048]{1,0:T(8,128)(2,1)}, ...), condition=%wide.region_3.5_spmd, body=%wide.region_2.4_spmd.sunk | while | flops 8388614 | bytes 599179 | solution.py:33
  24.6 1.3 fusion.72
  25.9 1.3 %fusion.72 = f32[16,1024]{1,0:T(8,128)S(1)} fusion(f32[16,1024]{1,0:T(8,128)S(1)} %get-tuple-element.184, s32[]{:T(128)S(6)} %select_n.118, bf16[16,2048]{1,0:T(8,128)(2,1)S(1)} %get-tuple-element.196, bf16[1024,2048]{1,0:T(8,128)(2,1)} %get-tuple-element.195), kind=kOutput, calls=%fused_computation.7.clone.1 | convolution fusion | flops 8388608 | bytes 599040 | tf_op jit(solution)/shard_map/while/body/dot_general | solution.py:28
  27.1 1.3 %fusion.72 = f32[16,1024]{1,0:T(8,128)S(1)} fusion(f32[16,1024]{1,0:T(8,128)S(1)} %get-tuple-element.184, s32[]{:T(128)S(6)} %select_n.118, bf16[16,2048]{1,0:T(8,128)(2,1)S(1)} %get-tuple-element.196, bf16[1024,2048]{1,0:T(8,128)(2,1)} %get-tuple-element.195), kind=kOutput, calls=%fused_computation.7.clone.1 | convolution fusion | flops 8388608 | bytes 599040 | tf_op jit(solution)/shard_map/while/body/dot_general | solution.py:28
  28.4 1.3 %fusion.72 = f32[16,1024]{1,0:T(8,128)S(1)} fusion(f32[16,1024]{1,0:T(8,128)S(1)} %get-tuple-element.184, s32[]{:T(128)S(6)} %select_n.118, bf16[16,2048]{1,0:T(8,128)(2,1)S(1)} %get-tuple-element.196, bf16[1024,2048]{1,0:T(8,128)(2,1)} %get-tuple-element.195), kind=kOutput, calls=%fused_computation.7.clone.1 | convolution fusion | flops 8388608 | bytes 599040 | tf_op jit(solution)/shard_map/while/body/dot_general | solution.py:28
  29.7 1.3 %fusion.72 = f32[16,1024]{1,0:T(8,128)S(1)} fusion(f32[16,1024]{1,0:T(8,128)S(1)} %get-tuple-element.184, s32[]{:T(128)S(6)} %select_n.118, bf16[16,2048]{1,0:T(8,128)(2,1)S(1)} %get-tuple-element.196, bf16[1024,2048]{1,0:T(8,128)(2,1)} %get-tuple-element.195), kind=kOutput, calls=%fused_computation.7.clone.1 | convolution fusion | flops 8388608 | bytes 599040 | tf_op jit(solution)/shard_map/while/body/dot_general | solution.py:28
  31.0 1.3 %fusion.72 = f32[16,1024]{1,0:T(8,128)S(1)} fusion(f32[16,1024]{1,0:T(8,128)S(1)} %get-tuple-element.184, s32[]{:T(128)S(6)} %select_n.118, bf16[16,2048]{1,0:T(8,128)(2,1)S(1)} %get-tuple-element.196, bf16[1024,2048]{1,0:T(8,128)(2,1)} %get-tuple-element.195), kind=kOutput, calls=%fused_computation.7.clone.1 | convolution fusion | flops 8388608 | bytes 599040 | tf_op jit(solution)/shard_map/while/body/dot_general | solution.py:28
  32.3 1.3 %fusion.72 = f32[16,1024]{1,0:T(8,128)S(1)} fusion(f32[16,1024]{1,0:T(8,128)S(1)} %get-tuple-element.184, s32[]{:T(128)S(6)} %select_n.118, bf16[16,2048]{1,0:T(8,128)(2,1)S(1)} %get-tuple-element.196, bf16[1024,2048]{1,0:T(8,128)(2,1)} %get-tuple-element.195), kind=kOutput, calls=%fused_computation.7.clone.1 | convolution fusion | flops 8388608 | bytes 599040 | tf_op jit(solution)/shard_map/while/body/dot_general | solution.py:28
  33.6 1.3 %fusion.72 = f32[16,1024]{1,0:T(8,128)S(1)} fusion(f32[16,1024]{1,0:T(8,128)S(1)} %get-tuple-element.184, s32[]{:T(128)S(6)} %select_n.118, bf16[16,2048]{1,0:T(8,128)(2,1)S(1)} %get-tuple-element.196, bf16[1024,2048]{1,0:T(8,128)(2,1)} %get-tuple-element.195), kind=kOutput, calls=%fused_computation.7.clone.1 | convolution fusion | flops 8388608 | bytes 599040 | tf_op jit(solution)/shard_map/while/body/dot_general | solution.py:28
  35.3 5.0 %psum.57 = f32[16,48]{1,0:T(8,128)S(1)} all-reduce(f32[16,48]{1,0:T(8,128)S(1)} %fusion.30), channel_id=1, replica_groups=mesh['parts'=2,'sub'=4,'row'=2,'col'=2] {'row'}, use_global_device_ids=true, to_apply=%region_4.6 | all-reduce | flops 768 | bytes 6144 | tf_op jit(solution)/shard_map/psum | solution.py:83
  40.2 10.1 %psum.58 = f32[16,48]{1,0:T(8,128)S(1)} all-reduce(f32[16,48]{1,0:T(8,128)S(1)} %psum.57), channel_id=1, replica_groups=mesh['parts'=2,'sub'=4,'row'=2,'col'=2] {'sub'}, use_global_device_ids=true, to_apply=%region_5.7 | all-reduce | flops 768 | bytes 6144 | tf_op jit(solution)/shard_map/psum | solution.py:83
  50.9 4.6 %all_gather.6 = bf16[16,2048]{1,0:T(8,128)(2,1)S(1)} all-gather(bf16[16,1024]{1,0:T(8,128)(2,1)S(1)} %fusion.6), channel_id=1, replica_groups=mesh['parts'=2,'sub'=4,'row'=2,'col'=2] {'row'}, dimensions={1}, use_global_device_ids=true | all-gather | bytes 98304 | tf_op jit(solution)/shard_map/all_gather | solution.py:89
  55.8 3.5 %collective-permute-start.3 = (bf16[16,1024]{1,0:T(8,128)(2,1)S(1)}, bf16[16,1024]{1,0:T(8,128)(2,1)S(1)}, u32[]{:S(2)}, u32[]{:S(2)}) collective-permute-start(bf16[16,1024]{1,0:T(8,128)(2,1)S(1)} %get-tuple-element.103), channel_id=1, source_target_pairs={{0,12},{4,0},{8,4},{12,8},{1,13},{5,1},{9,5},{13,9},{2,14},{6,2},{... | collective-permute-start | bytes 98312 | tf_op jit(solution)/shard_map/ppermute | solution.py:13
  59.3 1.9 %collective-permute-done.2 = bf16[16,1024]{1,0:T(8,128)(2,1)S(1)} collective-permute-done((bf16[16,1024]{1,0:T(8,128)(2,1)S(1)}, bf16[16,1024]{1,0:T(8,128)(2,1)S(1)}, u32[]{:S(2)}, u32[]{:S(2)}) %collective-permute-start.2) | collective-permute-done | bytes 32800 | tf_op jit(solution)/shard_map/ppermute | solution.py:13
  61.3 2.8 %gather_fusion.2 = f32[1024,16]{1,0:T(8,128)S(1)} fusion(f32[16,1024]{0,1:T(8,128)S(1)} %copy.23, s32[1024]{0:T(1024)S(1)} %fusion.37), kind=kCustom, calls=%fused_computation.1.clone | custom fusion | bytes 135168 | tf_op jit(solution)/shard_map/jit(_take)/gather | solution.py:96
  64.4 2.8 %gather_fusion.3 = f32[1024,16]{1,0:T(8,128)S(1)} fusion(f32[16,1024]{0,1:T(8,128)S(1)} %copy.25, s32[1024]{0:T(1024)S(1)} %fusion.36), kind=kCustom, calls=%fused_computation.2.clone | custom fusion | bytes 135168 | tf_op jit(solution)/shard_map/jit(_take)/gather | solution.py:97
  67.6 9.1 %all-reduce.1 = (f32[16]{0:T(128)S(1)}, f32[16]{0:T(128)S(1)}) all-reduce(f32[16]{0:T(128)S(1)} %get-tuple-element.64, f32[16]{0:T(128)S(1)} %get-tuple-element.63), channel_id=1, replica_groups=mesh['parts'=2,'sub'=4,'row'=2,'col'=2] {'sub'}, use_global_device_ids=true, to_apply=%region_1.3 | all-reduce | flops 32 | bytes 256 | tf_op jit(solution)/shard_map/psum | solution.py:21
  76.9 10.3 %while.21 = (s32[]{:T(128)}, f32[16,1024]{1,0:T(8,128)S(1)}, s32[]{:T(128)}, bf16[1024,2048]{1,0:T(8,128)(2,1)}, bf16[16,2048]{1,0:T(8,128)(2,1)S(1)}, /*index=5*/s32[]{:T(128)}, s32[]{:T(128)}, s32[]{:T(128)}, s32[]{:T(128)}) while((s32[]{:T(128)}, f32[16,1024]{1,0:T(8,128)S(1)}, s32[]{:T(128)}, bf16[1024,2048]{1,0:T(8,128)(2,1)}, ...), condition=%wide.region_11.13_spmd, body=%wide.region_10.12_spmd.sunk | while | flops 8388614 | bytes 599179 | solution.py:33
  76.9 1.3 fusion.75
  78.1 1.3 %fusion.75 = f32[16,1024]{1,0:T(8,128)S(1)} fusion(f32[16,1024]{1,0:T(8,128)S(1)} %get-tuple-element.211, s32[]{:T(128)S(6)} %select_n.119, bf16[16,2048]{1,0:T(8,128)(2,1)S(1)} %get-tuple-element.223, bf16[1024,2048]{1,0:T(8,128)(2,1)} %get-tuple-element.222), kind=kOutput, calls=%fused_computation.11.clone.1 | convolution fusion | flops 8388608 | bytes 599040 | tf_op jit(solution)/shard_map/while/body/dot_general | solution.py:28
  79.4 1.3 %fusion.75 = f32[16,1024]{1,0:T(8,128)S(1)} fusion(f32[16,1024]{1,0:T(8,128)S(1)} %get-tuple-element.211, s32[]{:T(128)S(6)} %select_n.119, bf16[16,2048]{1,0:T(8,128)(2,1)S(1)} %get-tuple-element.223, bf16[1024,2048]{1,0:T(8,128)(2,1)} %get-tuple-element.222), kind=kOutput, calls=%fused_computation.11.clone.1 | convolution fusion | flops 8388608 | bytes 599040 | tf_op jit(solution)/shard_map/while/body/dot_general | solution.py:28
  80.7 1.3 %fusion.75 = f32[16,1024]{1,0:T(8,128)S(1)} fusion(f32[16,1024]{1,0:T(8,128)S(1)} %get-tuple-element.211, s32[]{:T(128)S(6)} %select_n.119, bf16[16,2048]{1,0:T(8,128)(2,1)S(1)} %get-tuple-element.223, bf16[1024,2048]{1,0:T(8,128)(2,1)} %get-tuple-element.222), kind=kOutput, calls=%fused_computation.11.clone.1 | convolution fusion | flops 8388608 | bytes 599040 | tf_op jit(solution)/shard_map/while/body/dot_general | solution.py:28
  82.0 1.3 %fusion.75 = f32[16,1024]{1,0:T(8,128)S(1)} fusion(f32[16,1024]{1,0:T(8,128)S(1)} %get-tuple-element.211, s32[]{:T(128)S(6)} %select_n.119, bf16[16,2048]{1,0:T(8,128)(2,1)S(1)} %get-tuple-element.223, bf16[1024,2048]{1,0:T(8,128)(2,1)} %get-tuple-element.222), kind=kOutput, calls=%fused_computation.11.clone.1 | convolution fusion | flops 8388608 | bytes 599040 | tf_op jit(solution)/shard_map/while/body/dot_general | solution.py:28
  83.3 1.3 %fusion.75 = f32[16,1024]{1,0:T(8,128)S(1)} fusion(f32[16,1024]{1,0:T(8,128)S(1)} %get-tuple-element.211, s32[]{:T(128)S(6)} %select_n.119, bf16[16,2048]{1,0:T(8,128)(2,1)S(1)} %get-tuple-element.223, bf16[1024,2048]{1,0:T(8,128)(2,1)} %get-tuple-element.222), kind=kOutput, calls=%fused_computation.11.clone.1 | convolution fusion | flops 8388608 | bytes 599040 | tf_op jit(solution)/shard_map/while/body/dot_general | solution.py:28
  84.6 1.3 %fusion.75 = f32[16,1024]{1,0:T(8,128)S(1)} fusion(f32[16,1024]{1,0:T(8,128)S(1)} %get-tuple-element.211, s32[]{:T(128)S(6)} %select_n.119, bf16[16,2048]{1,0:T(8,128)(2,1)S(1)} %get-tuple-element.223, bf16[1024,2048]{1,0:T(8,128)(2,1)} %get-tuple-element.222), kind=kOutput, calls=%fused_computation.11.clone.1 | convolution fusion | flops 8388608 | bytes 599040 | tf_op jit(solution)/shard_map/while/body/dot_general | solution.py:28
  85.9 1.3 %fusion.75 = f32[16,1024]{1,0:T(8,128)S(1)} fusion(f32[16,1024]{1,0:T(8,128)S(1)} %get-tuple-element.211, s32[]{:T(128)S(6)} %select_n.119, bf16[16,2048]{1,0:T(8,128)(2,1)S(1)} %get-tuple-element.223, bf16[1024,2048]{1,0:T(8,128)(2,1)} %get-tuple-element.222), kind=kOutput, calls=%fused_computation.11.clone.1 | convolution fusion | flops 8388608 | bytes 599040 | tf_op jit(solution)/shard_map/while/body/dot_general | solution.py:28
  87.4 5.0 %psum.61 = f32[16,48]{1,0:T(8,128)S(1)} all-reduce(f32[16,48]{1,0:T(8,128)S(1)} %fusion.29), channel_id=1, replica_groups=mesh['parts'=2,'sub'=4,'row'=2,'col'=2] {'row'}, use_global_device_ids=true, to_apply=%region_12.14 | all-reduce | flops 768 | bytes 6144 | tf_op jit(solution)/shard_map/psum | solution.py:83
  92.4 9.8 %psum.62 = f32[16,48]{1,0:T(8,128)S(1)} all-reduce(f32[16,48]{1,0:T(8,128)S(1)} %psum.61), channel_id=1, replica_groups=mesh['parts'=2,'sub'=4,'row'=2,'col'=2] {'sub'}, use_global_device_ids=true, to_apply=%region_13.15 | all-reduce | flops 768 | bytes 6144 | tf_op jit(solution)/shard_map/psum | solution.py:83
  102.7 4.6 %all_gather.7 = bf16[16,2048]{1,0:T(8,128)(2,1)S(1)} all-gather(bf16[16,1024]{1,0:T(8,128)(2,1)S(1)} %fusion.7), channel_id=1, replica_groups=mesh['parts'=2,'sub'=4,'row'=2,'col'=2] {'row'}, dimensions={1}, use_global_device_ids=true | all-gather | bytes 98304 | tf_op jit(solution)/shard_map/all_gather | solution.py:89
  107.3 0.7 collective-permute-start.5
  108.0 1.3 %collective-permute-start.4 = (bf16[16,1024]{1,0:T(8,128)(2,1)S(1)}, bf16[16,1024]{1,0:T(8,128)(2,1)S(1)}, u32[]{:S(2)}, u32[]{:S(2)}) collective-permute-start(bf16[16,1024]{1,0:T(8,128)(2,1)S(1)} %get-tuple-element.101), channel_id=1, source_target_pairs={{0,4},{4,8},{8,12},{12,0},{1,5},{5,9},{9,13},{13,1},{2,6},{6,10},{... | collective-permute-start | bytes 98312 | tf_op jit(solution)/shard_map/ppermute | solution.py:13
  109.3 1.9 %collective-permute-done.5 = bf16[16,1024]{1,0:T(8,128)(2,1)S(1)} collective-permute-done((bf16[16,1024]{1,0:T(8,128)(2,1)S(1)}, bf16[16,1024]{1,0:T(8,128)(2,1)S(1)}, u32[]{:S(2)}, u32[]{:S(2)}) %collective-permute-start.5) | collective-permute-done | bytes 32800 | tf_op jit(solution)/shard_map/ppermute | solution.py:13
  111.3 2.8 %gather_fusion.5 = f32[1024,16]{1,0:T(8,128)S(1)} fusion(f32[16,1024]{0,1:T(8,128)S(1)} %copy.29, s32[1024]{0:T(1024)S(1)} %fusion.36), kind=kCustom, calls=%fused_computation.4.clone | custom fusion | bytes 135168 | tf_op jit(solution)/shard_map/jit(_take)/gather | solution.py:97
  114.5 2.8 %gather_fusion.4 = f32[1024,16]{1,0:T(8,128)S(1)} fusion(f32[16,1024]{0,1:T(8,128)S(1)} %copy.27, s32[1024]{0:T(1024)S(1)} %fusion.37), kind=kCustom, calls=%fused_computation.3.clone | custom fusion | bytes 135168 | tf_op jit(solution)/shard_map/jit(_take)/gather | solution.py:96
  117.6 10.9 %all-reduce = (f32[16]{0:T(128)S(1)}, f32[16]{0:T(128)S(1)}) all-reduce(f32[16]{0:T(128)S(1)} %get-tuple-element.62, f32[16]{0:T(128)S(1)} %get-tuple-element.61), channel_id=1, replica_groups=mesh['parts'=2,'sub'=4,'row'=2,'col'=2] {'sub'}, use_global_device_ids=true, to_apply=%region_9.11 | all-reduce | flops 32 | bytes 256 | tf_op jit(solution)/shard_map/psum | solution.py:21
  128.5 0.7 fusion.16
  (57 shorter events, 5.2 us)
Async XLA Ops:
  0.6 34.3 %copy-start = (bf16[1,24,1024]{2,1,0:T(8,128)(2,1)S(1)}, bf16[1,24,1024]{2,1,0:T(8,128)(2,1)}, u32[]{:S(2)}) copy-start(bf16[1,24,1024]{2,1,0:T(8,128)(2,1)} %param.18) | copy-start | bytes 147460
  0.6 20.7 %copy-start.5 = (f32[1,1024]{1,0:T(1,128)S(1)}, f32[1,1024]{1,0:T(1,128)}, u32[]{:S(2)}) copy-start(f32[1,1024]{1,0:T(1,128)} %param.16) | copy-start | bytes 12292
  0.7 20.6 %copy-start.2 = (s32[1,1024]{1,0:T(1,128)S(1)}, s32[1,1024]{1,0:T(1,128)}, u32[]{:S(2)}) copy-start(s32[1,1024]{1,0:T(1,128)} %param.23) | copy-start | bytes 12292
  1.5 19.8 %collective-permute-start.1 = (bf16[16,1024]{1,0:T(8,128)(2,1)S(1)}, bf16[16,1024]{1,0:T(8,128)(2,1)S(1)}, u32[]{:S(2)}, u32[]{:S(2)}) collective-permute-start(bf16[16,1024]{1,0:T(8,128)(2,1)S(1)} %bitcast_convert_fusion), channel_id=1, source_target_pairs={{0,12},{4,0},{8,4},{12,8},{1,13},{5,1},{9,5},{13,9},{2,14},{6,2},{... | collective-permute-start | bytes 98312 | tf_op jit(solution)/shard_map/ppermute | solution.py:13
  7.3 9.4 %collective-permute-start = (bf16[1,1024]{1,0:T(2,128)(2,1)S(1)}, bf16[1,1024]{1,0:T(2,128)(2,1)S(1)}, u32[]{:S(2)}, u32[]{:S(2)}) collective-permute-start(bf16[1,1024]{1,0:T(2,128)(2,1)S(1)} %convert_element_type.71), channel_id=1, source_target_pairs={{0,12},{4,0},{8,4},{12,8},{1,13},{5,1},{9,5},{13,9},{2,14},{6,2},{... | collective-permute-start | bytes 6152 | tf_op jit(solution)/shard_map/ppermute | solution.py:13
  16.7 33.6 %copy-start.3 = (f32[48,48]{1,0:T(8,128)S(1)}, f32[48,48]{1,0:T(8,128)}, u32[]{:S(2)}) copy-start(f32[48,48]{1,0:T(8,128)} %param.19) | copy-start | bytes 27652
  16.7 42.5 %copy-start.4 = (s32[1,1024]{1,0:T(1,128)S(1)}, s32[1,1024]{1,0:T(1,128)}, u32[]{:S(2)}) copy-start(s32[1,1024]{1,0:T(1,128)} %param.22) | copy-start | bytes 12292
  24.5 42.9 %copy-start.1 = (f32[1,16,1024]{2,1,0:T(8,128)S(1)}, f32[1,16,1024]{2,1,0:T(8,128)}, u32[]{:S(2)}) copy-start(f32[1,16,1024]{2,1,0:T(8,128)} %param.15) | copy-start | bytes 196612
  55.4 5.7 %collective-permute-start.2 = (bf16[16,1024]{1,0:T(8,128)(2,1)S(1)}, bf16[16,1024]{1,0:T(8,128)(2,1)S(1)}, u32[]{:S(2)}, u32[]{:S(2)}) collective-permute-start(bf16[16,1024]{1,0:T(8,128)(2,1)S(1)} %get-tuple-element.102), channel_id=1, source_target_pairs={{0,4},{4,8},{8,12},{12,0},{1,5},{5,9},{9,13},{13,1},{2,6},{6,10},{... | collective-permute-start | bytes 98312 | tf_op jit(solution)/shard_map/ppermute | solution.py:13
  55.8 8.5 %collective-permute-start.3 = (bf16[16,1024]{1,0:T(8,128)(2,1)S(1)}, bf16[16,1024]{1,0:T(8,128)(2,1)S(1)}, u32[]{:S(2)}, u32[]{:S(2)}) collective-permute-start(bf16[16,1024]{1,0:T(8,128)(2,1)S(1)} %get-tuple-element.103), channel_id=1, source_target_pairs={{0,12},{4,0},{8,4},{12,8},{1,13},{5,1},{9,5},{13,9},{2,14},{6,2},{... | collective-permute-start | bytes 98312 | tf_op jit(solution)/shard_map/ppermute | solution.py:13
  107.3 3.9 %collective-permute-start.5 = (bf16[16,1024]{1,0:T(8,128)(2,1)S(1)}, bf16[16,1024]{1,0:T(8,128)(2,1)S(1)}, u32[]{:S(2)}, u32[]{:S(2)}) collective-permute-start(bf16[16,1024]{1,0:T(8,128)(2,1)S(1)} %get-tuple-element.100), channel_id=1, source_target_pairs={{0,12},{4,0},{8,4},{12,8},{1,13},{5,1},{9,5},{13,9},{2,14},{6,2},{... | collective-permute-start | bytes 98312 | tf_op jit(solution)/shard_map/ppermute | solution.py:13
  108.0 6.3 %collective-permute-start.4 = (bf16[16,1024]{1,0:T(8,128)(2,1)S(1)}, bf16[16,1024]{1,0:T(8,128)(2,1)S(1)}, u32[]{:S(2)}, u32[]{:S(2)}) collective-permute-start(bf16[16,1024]{1,0:T(8,128)(2,1)S(1)} %get-tuple-element.101), channel_id=1, source_target_pairs={{0,4},{4,8},{8,12},{12,0},{1,5},{5,9},{9,13},{13,1},{2,6},{6,10},{... | collective-permute-start | bytes 98312 | tf_op jit(solution)/shard_map/ppermute | solution.py:13
